TPU v7x, 512 devices: a whole 4x4x16 slice. The times are simulated.
512 devices in a mesh: hour: 16 (over z), dom: 32 (over x, y, core).
Axes of the slice: x: 4, y: 4, z: 16, core: 2. Of those that a mesh axis runs over, the one named last changes fastest.
Arguments:
- query_matrix: bfloat16 [16, 4096, 1024], P('hour', 'dom'), may hold values from -1.6953125 to 1.6953125
- key_matrix: bfloat16 [16, 4096, 1024], P('hour', 'dom'), may hold values from -1.6953125 to 1.6953125
- value_matrix: bfloat16 [16, 4096, 1024], P('hour', 'dom'), may hold values from -6 to 6
- saved_output: bfloat16 [16, 4096, 1024], P('hour', 'dom'), may hold values from -6 to 6
- output_grad: bfloat16 [16, 4096, 1024], P('hour', 'dom'), may hold values from -16 to 16
- row_logsum: float32 [16, 16, 4096], P('hour', None, 'dom'), may hold values from 5.7 to 6.7
- key_blocks: int32 [32, 1], P('dom'), may hold values from 0 to 1, as said below
- halo_rows: int32 [32, 32, 4], replicated, may hold values from -1 to 127, as said below
Outputs:
- query_grad: bfloat16 [16, 4096, 1024], P('hour', 'dom')
- key_grad: bfloat16 [16, 4096, 1024], P('hour', 'dom')
- value_grad: bfloat16 [16, 4096, 1024], P('hour', 'dom')
Inputs may be any that keep to these rules, and one draw needn't show every extreme that they name: `key_blocks`: row d + b holds 1 distinct candidate blocks in increasing order for query block b of partition d. `halo_rows`: entry [d, p, c] is the row, within partition p, that partition d receives in slot c, or -1 for an empty slot. No partition receives from itself; from each partition the live slots come first; partition d receives 4 live rows from partition (d + 1) % 32; entry c lies in rows c * (32) to (c + 1) * 32 - 1.
All inputs are finite; a program needn't handle non-finite values.
Results may differ from a plain program's by a relative error of at most 0.0049.
Values may be sent and summed in bfloat16 or wider, within the bound.
No kernel may reach another device: no remote copies, remote signals or barrier semaphores. Data moves between devices by JAX's collectives and lax.ppermute only.
A program may use at most 64 MiB of HBM per device.

v0:
```python
import functools
import math

import jax
import jax.numpy as jnp
from jax import lax
from jax.experimental import pallas as pl
from jax.experimental.pallas import tpu as pltpu
from jax.sharding import PartitionSpec as P


BF = jnp.bfloat16
F32 = jnp.float32
LANES = 128
VMEM_LIMIT = 24 << 20


def dot(a, b):
    return lax.dot_general(a, b, (((1,), (0,)), ((), ())), preferred_element_type=F32)


def dot_nt(a, b):
    return lax.dot_general(a, b, (((1,), (1,)), ((), ())), preferred_element_type=F32)


def dot_tn(a, b):
    return lax.dot_general(a, b, (((0,), (0,)), ((), ())), preferred_element_type=F32)


def iota(shape, dim):
    return lax.broadcasted_iota(jnp.int32, shape, dim)


def one_where(mask):
    return jnp.where(mask, 1.0, 0.0).astype(BF)


def split3(x):
    hi = x.astype(BF)
    rest = x - hi.astype(F32)
    mid = rest.astype(BF)
    return hi, mid, (rest - mid.astype(F32)).astype(BF)


def start(triples):
    copies = [pltpu.make_async_copy(*triple) for triple in triples]
    for copy in copies:
        copy.start()
    return copies


def picks(halo, me, tokens, by_slot):
    rows = halo.astype(F32)
    table = rows.reshape(rows.shape[0] * rows.shape[1], rows.shape[2]).astype(BF)
    slots, owners = table.shape
    if by_slot:
        wanted = dot(table, one_where(iota((owners, tokens), 0) == me))
        return one_where(wanted.astype(jnp.int32) == iota((slots, tokens), 1))
    wanted = dot_nt(one_where(iota((tokens, owners), 1) == me), table)
    return one_where(wanted.astype(jnp.int32) == iota((tokens, slots), 0))


def front_kernel(
    me_ref,
    halo_hbm,
    query_hbm,
    key_hbm,
    value_hbm,
    cot_hbm,
    saved_hbm,
    logsum_hbm,
    pack_ref,
    extra_ref,
    send_hbm,
    halo_ref,
    saved_ref,
    logsum_ref,
    send_ref,
    sems,
):
    tokens, width = query_hbm.shape
    heads = logsum_hbm.shape[0]
    head_dim = width // heads
    domains, cap, _ = send_ref.shape
    pieces = [
        (halo_hbm, halo_ref),
        (key_hbm, pack_ref.at[:, 2 * width : 3 * width]),
        (value_hbm, pack_ref.at[:, 3 * width : 4 * width]),
        (cot_hbm, pack_ref.at[:, width : 2 * width]),
        (saved_hbm, saved_ref),
        (logsum_hbm, logsum_ref),
        (query_hbm, pack_ref.at[:, :width]),
    ]
    copies = start([(a, b, sems.at[i]) for i, (a, b) in enumerate(pieces)])
    copies[0].wait()
    pick = picks(halo_ref[...], me_ref[0], tokens, True)
    for i in (0, 1):
        copies[1 + i].wait()
        rows = dot(pick, pack_ref[:, (2 + i) * width : (3 + i) * width])
        send_ref[:, :, i * width : (i + 1) * width] = rows.reshape(domains, cap, width).astype(BF)
    outs = start([(send_ref, send_hbm, sems.at[len(pieces)])])
    for copy in copies[3:]:
        copy.wait()
    product = pack_ref[:, width : 2 * width].astype(F32) * saved_ref[...].astype(F32)
    high = product.astype(BF)
    low = (product - high.astype(F32)).astype(BF)
    member = one_where(iota((heads, width), 1) // head_dim == iota((heads, width), 0))
    delta = dot_nt(member, high) + dot_nt(member, low)
    parts = [p.astype(F32) for p in split3(logsum_ref[...]) + split3(delta)]
    parts.append(jnp.zeros((LANES - 6 * heads, tokens), F32))
    extra_ref[...] = jnp.concatenate(parts, axis=0).T.astype(BF)
    pack_ref[:, 4 * width :] = extra_ref[...]
    for copy in outs:
        copy.wait()


def extra_mask(head, heads, first):
    lane = iota((16, LANES), 1)
    inside = (lane >= first) & (lane < first + 3 * heads)
    return one_where(inside & (lane % heads == head))


def rows_of(pattern, tokens):
    return jnp.concatenate([pattern] * (tokens // pattern.shape[0]), axis=0)


def half_masks(tokens, head_dim):
    low = one_where(iota((16, LANES), 1) < head_dim)
    high = one_where(iota((16, LANES), 1) >= head_dim)
    return rows_of(low, tokens), rows_of(high, tokens)


def pair_dots(rows, row_extra, columns):
    return tuple(
        dot_nt(jnp.concatenate([row, extra], axis=1), column)
        for row, extra, column in zip(rows, row_extra, columns, strict=True)
    )


def pair_weights(dots, scale):
    score, grad = dots
    weight = jnp.exp2(score * (scale * math.log2(math.e)))
    return weight.astype(BF), (weight * grad).astype(BF)


def staged(count, first, second):
    ahead = first(0)
    for pair in range(count):
        now, ahead = ahead, first(pair + 1) if pair + 1 < count else None
        second(pair, now)


def minus_constants(rows, scale):
    return jnp.full((rows, LANES), -1.0 / scale, BF), jnp.full((rows, LANES), -1.0, BF)


def asking(query, cot, extra, pair, heads, masks):
    two_query, two_cot = two_heads(query, masks), two_heads(cot, masks)
    columns = (
        jnp.concatenate([two_query, two_extras(extra, pair, heads, 0)], axis=1),
        jnp.concatenate([two_cot, two_extras(extra, pair, heads, 3 * heads)], axis=1),
    )
    return two_query, two_cot, columns


def diagonal(product, tokens, head_dim):
    return jnp.concatenate([product[:head_dim, :tokens], product[head_dim:, tokens:]], axis=0)


def two_heads(block, masks):
    return jnp.concatenate([block * masks[0], block * masks[1]], axis=0)


def two_extras(extra, pair, heads, first):
    tokens = extra.shape[0]
    return jnp.concatenate(
        [extra * rows_of(extra_mask(2 * pair + i, heads, first), tokens) for i in (0, 1)], axis=0
    )


def halo_kernel(
    heads,
    block_ref,
    pack_ref,
    recv_ref,
    part_hbm,
    low_hbm,
    pool_hbm,
    back_hbm,
    pool,
    part,
    low,
    back,
    sems,
):
    tokens = pack_ref.shape[0]
    domains, cap, wide = recv_ref.shape
    width = wide // 2
    head_dim = width // heads
    scale = head_dim**-0.5
    local = block_ref[0] == 0

    @pl.when(local)
    def _():
        pool[:tokens] = pack_ref[:, 2 * width : 3 * width]
        pool[tokens:] = pack_ref[:, 3 * width : 4 * width]

    @pl.when(jnp.logical_not(local))
    def _():
        for i in (0, 1):
            rows = recv_ref[:, :, i * width : (i + 1) * width].astype(F32)
            pool[i * tokens : (i + 1) * tokens] = rows.reshape(domains * cap, width).astype(BF)

    outs = start([(pool.at[:tokens], pool_hbm, sems.at[0])])
    masks = half_masks(tokens, head_dim)
    constants = minus_constants(tokens, scale)
    to_own = jnp.where(local, 1.0, 0.0)
    to_halo = 1.0 - to_own

    def first(pair):
        at = pair * LANES
        query, cot = pack_ref[:, at : at + LANES], pack_ref[:, width + at : width + at + LANES]
        two_query, two_cot, columns = asking(
            query, cot, pack_ref[:, 4 * width :], pair, heads, masks
        )
        rows = pool[:tokens, at : at + LANES], pool[tokens:, at : at + LANES]
        return two_query, two_cot, pair_dots(rows, constants, columns)

    def second(pair, stage):
        at = pair * LANES
        two_query, two_cot, dots = stage
        weight_low, grad_low = pair_weights(dots, scale)
        low[:, 2 * at : 2 * at + 2 * LANES] = grad_low
        key_grad = dot(grad_low, two_query) * scale
        value_grad = dot(weight_low, two_cot)
        part[:tokens, at : at + LANES] = key_grad * to_own
        part[tokens:, at : at + LANES] = value_grad * to_own
        for i, grad in enumerate((key_grad, value_grad)):
            rows = (grad * to_halo).reshape(domains, cap, LANES)
            back[:, :, i * width + at : i * width + at + LANES] = rows.astype(BF)
        if pair % 4 != 3:
            return
        lanes = slice(at - 3 * LANES, at + LANES)
        wide = slice(2 * (at - 3 * LANES), 2 * (at + LANES))
        beside = slice(width + at - 3 * LANES, width + at + LANES)
        index = 4 * (pair // 4)
        outs.extend(
            start(
                [
                    (back.at[:, :, lanes], back_hbm.at[:, :, lanes], sems.at[index + 1]),
                    (back.at[:, :, beside], back_hbm.at[:, :, beside], sems.at[index + 2]),
                    (part.at[:, lanes], part_hbm.at[:, lanes], sems.at[index + 3]),
                    (low.at[:, wide], low_hbm.at[:, wide], sems.at[index + 4]),
                ]
            )
        )

    staged(heads // 2, first, second)
    for copy in outs:
        copy.wait()


def own_keys(keys, values, pair, heads, masks, scale):
    tokens = keys.shape[0]
    return tuple(
        jnp.concatenate(
            [
                two_heads(block, masks),
                jnp.concatenate(
                    [rows_of(extra_mask(2 * pair + i, heads, at) * BF(by), tokens) for i in (0, 1)],
                    axis=0,
                ),
            ],
            axis=1,
        )
        for block, at, by in ((keys, 0, -1.0 / scale), (values, 3 * heads, -1.0))
    )


def both_sides(heads, width, pack_ref, other, ready, before, finish):
    tokens = pack_ref.shape[0]
    head_dim = width // heads
    scale = head_dim**-0.5
    masks = half_masks(tokens, head_dim)
    constants = minus_constants(tokens, scale)

    def blocks(ref, pair):
        starts = [i * width + pair * LANES for i in range(4)]
        return [ref[:, at : at + LANES] for at in starts]

    def first(pair):
        ready(pair)
        query, cot, key, value = blocks(pack_ref, pair)
        their_query, their_cot, their_key, their_value = blocks(other, pair)
        extra = other[:, 4 * width :]
        _, _, columns = asking(query, cot, pack_ref[:, 4 * width :], pair, heads, masks)
        under = pair_dots(
            (their_query, their_cot), (extra, extra), own_keys(key, value, pair, heads, masks, scale)
        )
        over = pair_dots((their_key, their_value), constants, columns)
        return under, over

    def second(pair, stage):
        under, over = stage
        their_query, their_cot, their_key, _ = blocks(other, pair)
        weight_low, grad_low = pair_weights(under, scale)
        _, query_low = pair_weights(over, scale)
        keys, lows = before(pair, their_key, query_low)
        query_grad = diagonal(dot_tn(keys, lows), tokens, head_dim)
        key_grad = diagonal(dot_tn(their_query, grad_low), tokens, head_dim)
        value_grad = diagonal(dot_tn(their_cot, weight_low), tokens, head_dim)
        finish(pair, (query_grad * scale).T, (key_grad * scale).T, value_grad.T)

    staged(heads // 2, first, second)


def early_kernel(
    heads,
    me_ref,
    halo_hbm,
    pack_ref,
    other_hbm,
    low_hbm,
    pool_hbm,
    part_hbm,
    grads_hbm,
    place_ref,
    halo_ref,
    other,
    low,
    pool,
    part,
    grads,
    sems,
):
    tokens, width = pool_hbm.shape
    copies = start(
        [
            (other_hbm, other, sems.at[0]),
            (low_hbm, low, sems.at[1]),
            (pool_hbm, pool, sems.at[2]),
            (part_hbm, part, sems.at[3]),
            (halo_hbm, halo_ref, sems.at[4]),
        ]
    )
    copies[4].wait()
    place_ref[...] = picks(halo_ref[...], me_ref[0], tokens, False)
    copies[0].wait()
    outs = []

    def ready(pair):
        pass

    def before(pair, keys, query_low):
        if pair == 0:
            for copy in copies[1:4]:
                copy.wait()
        at = pair * LANES
        listed = low[:, 2 * at : 2 * at + 2 * LANES]
        return (
            jnp.concatenate([keys, pool[:, at : at + LANES]], axis=0),
            jnp.concatenate([query_low, listed], axis=0),
        )

    def finish(pair, query_grad, key_grad, value_grad):
        lanes = slice(pair * LANES, (pair + 1) * LANES)
        grads[:tokens, lanes] = query_grad
        grads[tokens : 2 * tokens, lanes] = part[:tokens, lanes] + key_grad
        grads[2 * tokens :, lanes] = part[tokens:, lanes] + value_grad
        if pair % 4 == 3:
            done = slice((pair - 3) * LANES, (pair + 1) * LANES)
            outs.extend(
                start([(grads.at[:, done], grads_hbm.at[:, done], sems.at[5 + pair // 4])])
            )

    both_sides(heads, width, pack_ref, other, ready, before, finish)
    for copy in outs:
        copy.wait()


def late_kernel(
    heads,
    own_query_hbm,
    own_cot_hbm,
    own_key_hbm,
    own_value_hbm,
    extra_ref,
    other_hbm,
    grads_hbm,
    total_ref,
    query_hbm,
    own,
    other,
    grads,
    query_ref,
    sems,
):
    tokens, width = query_hbm.shape
    half = width // 2

    def load(side):
        owned = (own_query_hbm, own_cot_hbm, own_key_hbm, own_value_hbm)
        part = slice(side * half, (side + 1) * half)
        blocks = [slice(i * width + side * half, i * width + (side + 1) * half) for i in range(4)]
        at = 9 * side
        triples = [
            (other_hbm.at[:, block], other.at[:, block], sems.at[at + i])
            for i, block in enumerate(blocks)
        ]
        triples += [
            (hbm.at[:, part], own.at[:, block], sems.at[at + 4 + i])
            for i, (hbm, block) in enumerate(zip(owned, blocks, strict=True))
        ]
        triples.append((grads_hbm.at[:, part], grads.at[:, part], sems.at[at + 8]))
        return start(triples)

    beside = slice(4 * width, 4 * width + LANES)
    extra = start([(other_hbm.at[:, beside], other.at[:, beside], sems.at[18])])
    copies = load(0), load(1)
    own[:, 4 * width :] = extra_ref[...]
    outs = []

    def ready(pair):
        if pair == 0:
            for copy in extra + copies[0][:8]:
                copy.wait()
        if pair == heads // 4:
            for copy in copies[1][:8]:
                copy.wait()

    def before(pair, keys, query_low):
        if pair == 0:
            copies[0][8].wait()
            copies[1][8].wait()
        return keys, query_low

    def finish(pair, query_grad, key_grad, value_grad):
        lanes = slice(pair * LANES, (pair + 1) * LANES)
        query_ref[:, lanes] = (grads[:tokens, lanes] + query_grad).astype(BF)
        total_ref[:tokens, lanes] = grads[tokens : 2 * tokens, lanes] + key_grad
        total_ref[tokens:, lanes] = grads[2 * tokens :, lanes] + value_grad
        if pair % 4 == 3:
            done = slice((pair - 3) * LANES, (pair + 1) * LANES)
            outs.extend(
                start([(query_ref.at[:, done], query_hbm.at[:, done], sems.at[19 + pair // 4])])
            )

    both_sides(heads, width, own, other, ready, before, finish)
    for copy in outs:
        copy.wait()


def scatter_kernel(place_ref, returned_ref, total_ref, key_hbm, value_hbm, out_ref, sems):
    tokens, width = key_hbm.shape
    domains, cap, _ = returned_ref.shape
    outs = []
    chunk = 4 * LANES
    for i in range(width // chunk):
        for j, hbm in enumerate((key_hbm, value_hbm)):
            lanes = slice(i * chunk, (i + 1) * chunk)
            rows = slice(j * tokens, (j + 1) * tokens)
            at = j * width + i * chunk
            returned = returned_ref[:, :, at : at + chunk].astype(F32)
            returned = returned.reshape(domains * cap, chunk).astype(BF)
            out_ref[rows, lanes] = (total_ref[rows, lanes] + dot(place_ref[...], returned)).astype(BF)
            outs += start([(out_ref.at[rows, lanes], hbm.at[:, lanes], sems.at[2 * i + j])])
    for copy in outs:
        copy.wait()


SMEM, VMEM, HBM = pltpu.SMEM, pltpu.VMEM, pltpu.HBM


def call(kernel, ins, outs, cost, scratch, sems):
    run = pl.pallas_call(
        kernel,
        out_shape=tuple(space(shape, kind) for shape, kind, space in outs),
        in_specs=[pl.BlockSpec(memory_space=space) for space in ins],
        out_specs=tuple(pl.BlockSpec(memory_space=space) for _, _, space in outs),
        scratch_shapes=[pltpu.VMEM(*s) for s in scratch] + [pltpu.SemaphoreType.DMA((sems,))],
        compiler_params=pltpu.CompilerParams(vmem_limit_bytes=VMEM_LIMIT),
        cost_estimate=pl.CostEstimate(flops=cost[0], bytes_accessed=cost[1], transcendentals=0),
    )

    def placed(*args):
        return run(
            *(
                pltpu.with_memory_space_constraint(x, space) if space is HBM else x
                for x, space in zip(args, ins, strict=True)
            )
        )

    return placed


def swap(block, axis, first):
    size = lax.axis_size(axis)
    pairs = [(i, i + 1) for i in range(first, size - 1, 2)]
    return lax.ppermute(block, axis, pairs + [(b, a) for a, b in pairs])


def backward(
    query_matrix,
    key_matrix,
    value_matrix,
    saved_output,
    output_grad,
    row_logsum,
    key_blocks,
    halo_rows,
):
    queries, keys, values = query_matrix[0], key_matrix[0], value_matrix[0]
    saved, cotangent, logsum = saved_output[0], output_grad[0], row_logsum[0]
    tokens, width = queries.shape
    heads = logsum.shape[0]
    domains, _, cap = halo_rows.shape
    slots = domains * cap
    me = lax.axis_index("dom").astype(jnp.int32).reshape(1)
    halo = halo_rows.transpose(0, 2, 1)
    array = tokens * width
    packed = 4 * width + LANES

    def exchange(block):
        return lax.all_to_all(block, "dom", split_axis=0, concat_axis=0, tiled=True)

    pack, extra, send = call(
        front_kernel,
        (SMEM,) + (HBM,) * 7,
        (
            ((tokens, packed), BF, VMEM),
            ((tokens, LANES), BF, VMEM),
            ((domains, cap, 2 * width), BF, HBM),
        ),
        (2 * slots * array, 20 * array),
        (
            (halo.shape, jnp.int32),
            ((tokens, width), BF),
            (logsum.shape, F32),
            ((domains, cap, 2 * width), BF),
        ),
        8,
    )(me, halo, queries, keys, values, cotangent, saved, logsum)
    received = exchange(send)
    odd = swap(pack, "hour", 1)
    even = swap(pack, "hour", 0)
    part, low, pool, back = call(
        functools.partial(halo_kernel, heads),
        (SMEM, VMEM, VMEM),
        (
            ((2 * tokens, width), F32, HBM),
            ((tokens, 2 * width), BF, HBM),
            ((tokens, width), BF, HBM),
            ((domains, cap, 2 * width), BF, HBM),
        ),
        (20 * tokens * array, 30 * array),
        (
            ((2 * tokens, width), BF),
            ((2 * tokens, width), F32),
            ((tokens, 2 * width), BF),
            ((domains, cap, 2 * width), BF),
        ),
        1 + heads // 2,
    )(key_blocks.reshape(1), pack, received)
    returned = exchange(back)
    grads, place = call(
        functools.partial(early_kernel, heads),
        (SMEM, HBM, VMEM, pl.ANY, HBM, HBM, HBM),
        (((3 * tokens, width), F32, HBM), ((tokens, slots), BF, VMEM)),
        (30 * tokens * array, 40 * array),
        (
            (halo.shape, jnp.int32),
            ((tokens, packed), BF),
            ((tokens, 2 * width), BF),
            ((tokens, width), BF),
            ((2 * tokens, width), F32),
            ((3 * tokens, width), F32),
        ),
        5 + heads // 8,
    )(me, halo, pack, even, low, pool, part)
    total, query_grad = call(
        functools.partial(late_kernel, heads),
        (HBM, HBM, HBM, HBM, VMEM, pl.ANY, HBM),
        (((2 * tokens, width), F32, VMEM), ((tokens, width), BF, HBM)),
        (28 * tokens * array, 40 * array),
        (
            ((tokens, packed), BF),
            ((tokens, packed), BF),
            ((3 * tokens, width), F32),
            ((tokens, width), BF),
        ),
        19 + heads // 8,
    )(queries, cotangent, keys, values, extra, odd, grads)
    key_grad, value_grad = call(
        scatter_kernel,
        (VMEM, VMEM, VMEM),
        (((tokens, width), BF, HBM), ((tokens, width), BF, HBM)),
        (2 * slots * array, 16 * array),
        (((2 * tokens, width), BF),),
        2 * (width // (4 * LANES)),
    )(place, returned, total)
    return query_grad[None], key_grad[None], value_grad[None]


def solution(mesh):
    in_specs = (
        P("hour", "dom", None),
        P("hour", "dom", None),
        P("hour", "dom", None),
        P("hour", "dom", None),
        P("hour", "dom", None),
        P("hour", None, "dom"),
        P("dom", None),
        P(),
    )
    out_specs = (P("hour", "dom", None), P("hour", "dom", None), P("hour", "dom", None))
    return jax.shard_map(
        backward, mesh=mesh, in_specs=in_specs, out_specs=out_specs, check_vma=False
    )
```

profile of v0, /device:TPU:97, one launch (start us, length us, event | category | flops | bytes accessed | tf_op | source)
XLA Modules:
  0.0 49.9 jit_solution(3036289326490345292)
XLA Ops:
  0.6 2.4 %shard_map.103 = (bf16[128,4224]{1,0:T(8,128)(2,1)S(1)}, bf16[128,128]{1,0:T(8,128)(2,1)S(1)}, bf16[32,4,2048]{2,1,0:T(4,128)(2,1)}) custom-call(s32[1]{0:T(128)} %bitcast.4.me_ref, s32[32,4,32]{2,1,0:T(4,128)} %bitcast.21, bf16[128,1024]{1,0:T(8,128)(2,1)} %bitcast.13, bf16[128,1024]{1,0:T(8,128)(2,1)} %bitcast.17, bf16[128,1024]{1,0:T(8,128)(2,1)} %bitcast.19, ...), custom_call_target="tpu_custom_call" | custom-call | flops 33554432 | bytes 2621440 | tf_op jit(solution)/shard_map/pallas_call | solution.py:486
  3.0 1.9 %collective-permute-start.1 = (bf16[128,4224]{1,0:T(8,128)(2,1)S(1)}, bf16[128,4224]{1,0:T(8,128)(2,1)}, u32[]{:S(2)}, u32[]{:S(2)}) collective-permute-start(bf16[128,4224]{1,0:T(8,128)(2,1)S(1)} %get-tuple-element.17.pack_ref), channel_id=1, source_target_pairs={{0,32},{64,96},{128,160},{192,224},{256,288},{320,352},{384,416},{... | collective-permute-start | bytes 3244040 | tf_op jit(solution)/shard_map/ppermute | solution.py:499
  5.0 6.4 %collective-permute-start = (bf16[128,4224]{1,0:T(8,128)(2,1)S(1)}, bf16[128,4224]{1,0:T(8,128)(2,1)S(1)}, u32[]{:S(2)}, u32[]{:S(2)}) collective-permute-start(bf16[128,4224]{1,0:T(8,128)(2,1)S(1)} %get-tuple-element.17.pack_ref), channel_id=1, source_target_pairs={{32,64},{96,128},{160,192},{224,256},{288,320},{352,384},{416,448}... | collective-permute-start | bytes 3244040 | tf_op jit(solution)/shard_map/ppermute | solution.py:499
  11.3 8.3 %all-to-all-start = ((bf16[32,4,2048]{2,1,0:T(4,128)(2,1)}), bf16[32,4,2048]{2,1,0:T(4,128)(2,1)S(1)}, u32[]{:S(2)}, u32[]{:S(2)}) async-start(bf16[32,4,2048]{2,1,0:T(4,128)(2,1)} %get-tuple-element.18), calls=%async_computation | async-start | bytes 1048576 | tf_op jit(solution)/shard_map/all_to_all | solution.py:524
  20.3 10.9 %all-to-all-done.recv_ref = bf16[32,4,2048]{2,1,0:T(4,128)(2,1)S(1)} async-done(((bf16[32,4,2048]{2,1,0:T(4,128)(2,1)}), bf16[32,4,2048]{2,1,0:T(4,128)(2,1)S(1)}, u32[]{:S(2)}, u32[]{:S(2)}) %all-to-all-start) | async-done | bytes 524320 | tf_op jit(solution)/shard_map/all_to_all | solution.py:524
  31.3 2.4 %shard_map.104 = (f32[256,1024]{1,0:T(8,128)}, bf16[128,2048]{1,0:T(8,128)(2,1)}, bf16[128,1024]{1,0:T(8,128)(2,1)}, bf16[32,4,2048]{2,1,0:T(4,128)(2,1)}) custom-call(s32[1]{0:T(128)} %bitcast.12.block_ref, bf16[128,4224]{1,0:T(8,128)(2,1)S(1)} %get-tuple-element.17.pack_ref, bf16[32,4,2048]{2,1,0:T(4,128)(2,1)S(1)} %all-to-all-done.recv_ref), custom_call_target="tpu_custom_call" | custom-call | flops 335544320 | bytes 3932160 | tf_op jit(solution)/shard_map/pallas_call | solution.py:486
  33.6 3.7 %all-to-all-start.1 = ((bf16[32,4,2048]{2,1,0:T(4,128)(2,1)}), bf16[32,4,2048]{2,1,0:T(4,128)(2,1)S(1)}, u32[]{:S(2)}, u32[]{:S(2)}) async-start(bf16[32,4,2048]{2,1,0:T(4,128)(2,1)} %get-tuple-element.25), calls=%async_computation.1 | async-start | bytes 1048576 | tf_op jit(solution)/shard_map/all_to_all | solution.py:524
  37.3 0.0 collective-permute-done.1.other_hbm
  37.4 5.1 %shard_map.105 = (f32[384,1024]{1,0:T(8,128)}, bf16[128,128]{1,0:T(8,128)(2,1)S(1)}) custom-call(s32[1]{0:T(128)} %bitcast.4.me_ref, s32[32,4,32]{2,1,0:T(4,128)} %bitcast.22, bf16[128,4224]{1,0:T(8,128)(2,1)S(1)} %get-tuple-element.17.pack_ref, bf16[128,4224]{1,0:T(8,128)(2,1)} %collective-permute-done.1.other_hbm, ...), custom_call_target="tpu_custom_call" | custom-call | flops 503316480 | bytes 5242880 | tf_op jit(solution)/shard_map/pallas_call | solution.py:486
  42.4 0.0 collective-permute-done.other_hbm
  42.5 4.6 %shard_map.106 = (f32[256,1024]{1,0:T(8,128)S(1)}, bf16[128,1024]{1,0:T(8,128)(2,1)}) custom-call(bf16[128,1024]{1,0:T(8,128)(2,1)} %bitcast.14, bf16[128,1024]{1,0:T(8,128)(2,1)} %bitcast.16, bf16[128,1024]{1,0:T(8,128)(2,1)} %bitcast.18, bf16[128,1024]{1,0:T(8,128)(2,1)} %bitcast.20, bf16[128,128]{1,0:T(8,128)(2,1)S(1)} %get-tuple-element.16.extra_ref, ...), custom_call_target="tpu_custom_call" | custom-call | flops 469762048 | bytes 5242880 | tf_op jit(solution)/shard_map/pallas_call | solution.py:486
  47.1 1.8 %all-to-all-done.1.returned_ref = bf16[32,4,2048]{2,1,0:T(4,128)(2,1)S(1)} async-done(((bf16[32,4,2048]{2,1,0:T(4,128)(2,1)}), bf16[32,4,2048]{2,1,0:T(4,128)(2,1)S(1)}, u32[]{:S(2)}, u32[]{:S(2)}) %all-to-all-start.1) | async-done | bytes 524320 | tf_op jit(solution)/shard_map/all_to_all | solution.py:524
  48.9 1.0 %shard_map.107 = (bf16[128,1024]{1,0:T(8,128)(2,1)}, bf16[128,1024]{1,0:T(8,128)(2,1)}) custom-call(bf16[128,128]{1,0:T(8,128)(2,1)S(1)} %get-tuple-element.24.place_ref, bf16[32,4,2048]{2,1,0:T(4,128)(2,1)S(1)} %all-to-all-done.1.returned_ref, f32[256,1024]{1,0:T(8,128)S(1)} %get-tuple-element.26.total_ref), custom_call_target="tpu_custom_call" | custom-call | flops 33554432 | bytes 2097152 | tf_op jit(solution)/shard_map/pallas_call | solution.py:486
Async XLA Ops:
  3.0 34.3 %collective-permute-start.1 = (bf16[128,4224]{1,0:T(8,128)(2,1)S(1)}, bf16[128,4224]{1,0:T(8,128)(2,1)}, u32[]{:S(2)}, u32[]{:S(2)}) collective-permute-start(bf16[128,4224]{1,0:T(8,128)(2,1)S(1)} %get-tuple-element.17.pack_ref), channel_id=1, source_target_pairs={{0,32},{64,96},{128,160},{192,224},{256,288},{320,352},{384,416},{... | collective-permute-start | bytes 3244040 | tf_op jit(solution)/shard_map/ppermute | solution.py:499
  5.0 37.5 %collective-permute-start = (bf16[128,4224]{1,0:T(8,128)(2,1)S(1)}, bf16[128,4224]{1,0:T(8,128)(2,1)S(1)}, u32[]{:S(2)}, u32[]{:S(2)}) collective-permute-start(bf16[128,4224]{1,0:T(8,128)(2,1)S(1)} %get-tuple-element.17.pack_ref), channel_id=1, source_target_pairs={{32,64},{96,128},{160,192},{224,256},{288,320},{352,384},{416,448}... | collective-permute-start | bytes 3244040 | tf_op jit(solution)/shard_map/ppermute | solution.py:499
  11.3 19.9 %all-to-all-start = ((bf16[32,4,2048]{2,1,0:T(4,128)(2,1)}), bf16[32,4,2048]{2,1,0:T(4,128)(2,1)S(1)}, u32[]{:S(2)}, u32[]{:S(2)}) async-start(bf16[32,4,2048]{2,1,0:T(4,128)(2,1)} %get-tuple-element.18), calls=%async_computation | async-start | bytes 1048576 | tf_op jit(solution)/shard_map/all_to_all | solution.py:524
  33.6 15.3 %all-to-all-start.1 = ((bf16[32,4,2048]{2,1,0:T(4,128)(2,1)}), bf16[32,4,2048]{2,1,0:T(4,128)(2,1)S(1)}, u32[]{:S(2)}, u32[]{:S(2)}) async-start(bf16[32,4,2048]{2,1,0:T(4,128)(2,1)} %get-tuple-element.25), calls=%async_computation.1 | async-start | bytes 1048576 | tf_op jit(solution)/shard_map/all_to_all | solution.py:524
where the time goes:
time: 50.4 us; the launch traced here: 49.9 us
  starting transfers between devices  20.3 us (40%)
  Pallas kernels  15.5 us (31%)
  waiting for transfers between devices  12.8 us (25%)
  between operations  1.36 us (3%)
    pallas_call x5, Pallas kernels, placed(): run(*(pltpu.with_memory_space_constraint(x, space) if space is HBM else x...  15.5 us
    all_to_all x2, waiting for transfers between devices, exchange(): return lax.all_to_all(block, 'dom', split_axis=0, concat_axis=0, tiled=True)  12.8 us
    all_to_all x2, starting transfers between devices, exchange(): return lax.all_to_all(block, 'dom', split_axis=0, concat_axis=0, tiled=True)  12 us
    ppermute x2, starting transfers between devices, swap(): return lax.ppermute(block, axis, pairs + [(b, a) for a, b in pairs])  8.3 us
  transfers between devices with their start and end apart: 4, of which 2 were waited for; matrix products, arithmetic and copies ran while one was open for 0% of the time, Pallas kernels for 24%

commit v1 on v0

--- a/solution.py
+++ b/solution.py
@@ -387,15 +387,19 @@
     extra_ref,
     other_hbm,
     grads_hbm,
-    total_ref,
+    place_ref,
+    returned_ref,
     query_hbm,
+    key_hbm,
+    value_hbm,
     own,
     other,
     grads,
-    query_ref,
+    result,
     sems,
 ):
     tokens, width = query_hbm.shape
+    domains, cap, _ = returned_ref.shape
     half = width // 2
 
     def load(side):
@@ -434,36 +438,31 @@
             copies[1][8].wait()
         return keys, query_low
 
+    def returned_rows(pair, i):
+        at = i * width + pair * LANES
+        rows = returned_ref[:, :, at : at + LANES].astype(F32)
+        return dot(place_ref[...], rows.reshape(domains * cap, LANES).astype(BF))
+
     def finish(pair, query_grad, key_grad, value_grad):
         lanes = slice(pair * LANES, (pair + 1) * LANES)
-        query_ref[:, lanes] = (grads[:tokens, lanes] + query_grad).astype(BF)
-        total_ref[:tokens, lanes] = grads[tokens : 2 * tokens, lanes] + key_grad
-        total_ref[tokens:, lanes] = grads[2 * tokens :, lanes] + value_grad
+        ends = query_grad, key_grad + returned_rows(pair, 0), value_grad + returned_rows(pair, 1)
+        rows = [slice(i * tokens, (i + 1) * tokens) for i in range(3)]
+        for row, end in zip(rows, ends, strict=True):
+            result[row, lanes] = (grads[row, lanes] + end).astype(BF)
         if pair % 4 == 3:
             done = slice((pair - 3) * LANES, (pair + 1) * LANES)
             outs.extend(
-                start([(query_ref.at[:, done], query_hbm.at[:, done], sems.at[19 + pair // 4])])
+                start(
+                    [
+                        (result.at[row, done], hbm.at[:, done], sems.at[19 + 3 * (pair // 4) + i])
+                        for i, (row, hbm) in enumerate(
+                            zip(rows, (query_hbm, key_hbm, value_hbm), strict=True)
+                        )
+                    ]
+                )
             )
 
     both_sides(heads, width, own, other, ready, before, finish)
-    for copy in outs:
-        copy.wait()
-
-
-def scatter_kernel(place_ref, returned_ref, total_ref, key_hbm, value_hbm, out_ref, sems):
-    tokens, width = key_hbm.shape
-    domains, cap, _ = returned_ref.shape
-    outs = []
-    chunk = 4 * LANES
-    for i in range(width // chunk):
-        for j, hbm in enumerate((key_hbm, value_hbm)):
-            lanes = slice(i * chunk, (i + 1) * chunk)
-            rows = slice(j * tokens, (j + 1) * tokens)
-            at = j * width + i * chunk
-            returned = returned_ref[:, :, at : at + chunk].astype(F32)
-            returned = returned.reshape(domains * cap, chunk).astype(BF)
-            out_ref[rows, lanes] = (total_ref[rows, lanes] + dot(place_ref[...], returned)).astype(BF)
-            outs += start([(out_ref.at[rows, lanes], hbm.at[:, lanes], sems.at[2 * i + j])])
     for copy in outs:
         copy.wait()
 
@@ -577,27 +576,19 @@
         ),
         5 + heads // 8,
     )(me, halo, pack, even, low, pool, part)
-    total, query_grad = call(
+    query_grad, key_grad, value_grad = call(
         functools.partial(late_kernel, heads),
-        (HBM, HBM, HBM, HBM, VMEM, pl.ANY, HBM),
-        (((2 * tokens, width), F32, VMEM), ((tokens, width), BF, HBM)),
-        (28 * tokens * array, 40 * array),
+        (HBM, HBM, HBM, HBM, VMEM, pl.ANY, HBM, VMEM, VMEM),
+        (((tokens, width), BF, HBM),) * 3,
+        (30 * tokens * array, 40 * array),
         (
             ((tokens, packed), BF),
             ((tokens, packed), BF),
             ((3 * tokens, width), F32),
-            ((tokens, width), BF),
+            ((3 * tokens, width), BF),
         ),
-        19 + heads // 8,
-    )(queries, cotangent, keys, values, extra, odd, grads)
-    key_grad, value_grad = call(
-        scatter_kernel,
-        (VMEM, VMEM, VMEM),
-        (((tokens, width), BF, HBM), ((tokens, width), BF, HBM)),
-        (2 * slots * array, 16 * array),
-        (((2 * tokens, width), BF),),
-        2 * (width // (4 * LANES)),
-    )(place, returned, total)
+        19 + 3 * (heads // 8),
+    )(queries, cotangent, keys, values, extra, odd, grads, place, returned)
     return query_grad[None], key_grad[None], value_grad[None]
 
 

time: 50.4 us -> 54.3 us (1.077)
  waiting for transfers between devices: 12.8 us -> 17.5 us
  Pallas kernels: 15.5 us -> 14.7 us
    all_to_all x2, waiting for transfers between devices: 12.8 us -> 17.5 us  [exchange(): return lax.all_to_all(block, 'dom', split_axis=0, concat_axis=0, tiled=True)]
    pallas_call x5 -> x4, Pallas kernels: 15.5 us -> 14.7 us  [placed(): run(*(pltpu.with_memory_space_constraint(x, space) if space is HBM else x...]
  transfers between devices with their start and end apart: 4 -> 4, of which waited for: 2 -> 2; matrix products, arithmetic and copies ran while one was open for 0% -> 0% of each run, Pallas kernels for 24% -> 14%
where the time goes in v1:
time: 54.3 us; the launch traced here: 53.9 us
  starting transfers between devices  20.3 us (37%)
  waiting for transfers between devices  17.5 us (32%)
  Pallas kernels  14.7 us (27%)
  between operations  1.35 us (2%)
    all_to_all x2, waiting for transfers between devices, exchange(): return lax.all_to_all(block, 'dom', split_axis=0, concat_axis=0, tiled=True)  17.5 us
    pallas_call x4, Pallas kernels, placed(): run(*(pltpu.with_memory_space_constraint(x, space) if space is HBM else x...  14.7 us
    all_to_all x2, starting transfers between devices, exchange(): return lax.all_to_all(block, 'dom', split_axis=0, concat_axis=0, tiled=True)  12 us
    ppermute x2, starting transfers between devices, swap(): return lax.ppermute(block, axis, pairs + [(b, a) for a, b in pairs])  8.3 us
  transfers between devices with their start and end apart: 4, of which 2 were waited for; matrix products, arithmetic and copies ran while one was open for 0% of the time, Pallas kernels for 14%

profile of v1, /device:TPU:97, one launch (start us, length us, event | category | flops | bytes accessed | tf_op | source)
XLA Modules:
  0.0 53.9 jit_solution(17847478975266303727)
XLA Ops:
  0.6 2.4 %shard_map.103 = (bf16[128,4224]{1,0:T(8,128)(2,1)S(1)}, bf16[128,128]{1,0:T(8,128)(2,1)S(1)}, bf16[32,4,2048]{2,1,0:T(4,128)(2,1)}) custom-call(s32[1]{0:T(128)} %bitcast.4.me_ref, s32[32,4,32]{2,1,0:T(4,128)} %bitcast.21, bf16[128,1024]{1,0:T(8,128)(2,1)} %bitcast.13, bf16[128,1024]{1,0:T(8,128)(2,1)} %bitcast.17, bf16[128,1024]{1,0:T(8,128)(2,1)} %bitcast.19, ...), custom_call_target="tpu_custom_call" | custom-call | flops 33554432 | bytes 2621440 | tf_op jit(solution)/shard_map/pallas_call | solution.py:485
  3.0 1.9 %collective-permute-start.1 = (bf16[128,4224]{1,0:T(8,128)(2,1)S(1)}, bf16[128,4224]{1,0:T(8,128)(2,1)}, u32[]{:S(2)}, u32[]{:S(2)}) collective-permute-start(bf16[128,4224]{1,0:T(8,128)(2,1)S(1)} %get-tuple-element.16.pack_ref), channel_id=1, source_target_pairs={{0,32},{64,96},{128,160},{192,224},{256,288},{320,352},{384,416},{... | collective-permute-start | bytes 3244040 | tf_op jit(solution)/shard_map/ppermute | solution.py:498
  5.0 6.4 %collective-permute-start = (bf16[128,4224]{1,0:T(8,128)(2,1)S(1)}, bf16[128,4224]{1,0:T(8,128)(2,1)S(1)}, u32[]{:S(2)}, u32[]{:S(2)}) collective-permute-start(bf16[128,4224]{1,0:T(8,128)(2,1)S(1)} %get-tuple-element.16.pack_ref), channel_id=1, source_target_pairs={{32,64},{96,128},{160,192},{224,256},{288,320},{352,384},{416,448}... | collective-permute-start | bytes 3244040 | tf_op jit(solution)/shard_map/ppermute | solution.py:498
  11.3 8.3 %all-to-all-start = ((bf16[32,4,2048]{2,1,0:T(4,128)(2,1)}), bf16[32,4,2048]{2,1,0:T(4,128)(2,1)S(1)}, u32[]{:S(2)}, u32[]{:S(2)}) async-start(bf16[32,4,2048]{2,1,0:T(4,128)(2,1)} %get-tuple-element.17), calls=%async_computation | async-start | bytes 1048576 | tf_op jit(solution)/shard_map/all_to_all | solution.py:523
  20.3 10.9 %all-to-all-done.recv_ref = bf16[32,4,2048]{2,1,0:T(4,128)(2,1)S(1)} async-done(((bf16[32,4,2048]{2,1,0:T(4,128)(2,1)}), bf16[32,4,2048]{2,1,0:T(4,128)(2,1)S(1)}, u32[]{:S(2)}, u32[]{:S(2)}) %all-to-all-start) | async-done | bytes 524320 | tf_op jit(solution)/shard_map/all_to_all | solution.py:523
  31.3 2.4 %shard_map.104 = (f32[256,1024]{1,0:T(8,128)}, bf16[128,2048]{1,0:T(8,128)(2,1)}, bf16[128,1024]{1,0:T(8,128)(2,1)}, bf16[32,4,2048]{2,1,0:T(4,128)(2,1)}) custom-call(s32[1]{0:T(128)} %bitcast.12.block_ref, bf16[128,4224]{1,0:T(8,128)(2,1)S(1)} %get-tuple-element.16.pack_ref, bf16[32,4,2048]{2,1,0:T(4,128)(2,1)S(1)} %all-to-all-done.recv_ref), custom_call_target="tpu_custom_call" | custom-call | flops 335544320 | bytes 3932160 | tf_op jit(solution)/shard_map/pallas_call | solution.py:485
  33.6 3.7 %all-to-all-start.1 = ((bf16[32,4,2048]{2,1,0:T(4,128)(2,1)}), bf16[32,4,2048]{2,1,0:T(4,128)(2,1)S(1)}, u32[]{:S(2)}, u32[]{:S(2)}) async-start(bf16[32,4,2048]{2,1,0:T(4,128)(2,1)} %get-tuple-element.23), calls=%async_computation.1 | async-start | bytes 1048576 | tf_op jit(solution)/shard_map/all_to_all | solution.py:523
  37.3 0.0 collective-permute-done.1.other_hbm
  37.4 5.0 %shard_map.105 = (f32[384,1024]{1,0:T(8,128)}, bf16[128,128]{1,0:T(8,128)(2,1)S(1)}) custom-call(s32[1]{0:T(128)} %bitcast.4.me_ref, s32[32,4,32]{2,1,0:T(4,128)} %bitcast.22, bf16[128,4224]{1,0:T(8,128)(2,1)S(1)} %get-tuple-element.16.pack_ref, bf16[128,4224]{1,0:T(8,128)(2,1)} %collective-permute-done.1.other_hbm, ...), custom_call_target="tpu_custom_call" | custom-call | flops 503316480 | bytes 5242880 | tf_op jit(solution)/shard_map/pallas_call | solution.py:485
  42.4 6.5 %all-to-all-done.1.returned_ref = bf16[32,4,2048]{2,1,0:T(4,128)(2,1)S(1)} async-done(((bf16[32,4,2048]{2,1,0:T(4,128)(2,1)}), bf16[32,4,2048]{2,1,0:T(4,128)(2,1)S(1)}, u32[]{:S(2)}, u32[]{:S(2)}) %all-to-all-start.1) | async-done | bytes 524320 | tf_op jit(solution)/shard_map/all_to_all | solution.py:523
  48.9 0.0 collective-permute-done.other_hbm
  48.9 4.9 %shard_map.106 = (bf16[128,1024]{1,0:T(8,128)(2,1)}, bf16[128,1024]{1,0:T(8,128)(2,1)}, bf16[128,1024]{1,0:T(8,128)(2,1)}) custom-call(bf16[128,1024]{1,0:T(8,128)(2,1)} %bitcast.14, bf16[128,1024]{1,0:T(8,128)(2,1)} %bitcast.16, bf16[128,1024]{1,0:T(8,128)(2,1)} %bitcast.18, bf16[128,1024]{1,0:T(8,128)(2,1)} %bitcast.20, ...), custom_call_target="tpu_custom_call" | custom-call | flops 503316480 | bytes 5242880 | tf_op jit(solution)/shard_map/pallas_call | solution.py:485
Async XLA Ops:
  3.0 34.3 %collective-permute-start.1 = (bf16[128,4224]{1,0:T(8,128)(2,1)S(1)}, bf16[128,4224]{1,0:T(8,128)(2,1)}, u32[]{:S(2)}, u32[]{:S(2)}) collective-permute-start(bf16[128,4224]{1,0:T(8,128)(2,1)S(1)} %get-tuple-element.16.pack_ref), channel_id=1, source_target_pairs={{0,32},{64,96},{128,160},{192,224},{256,288},{320,352},{384,416},{... | collective-permute-start | bytes 3244040 | tf_op jit(solution)/shard_map/ppermute | solution.py:498
  5.0 44.0 %collective-permute-start = (bf16[128,4224]{1,0:T(8,128)(2,1)S(1)}, bf16[128,4224]{1,0:T(8,128)(2,1)S(1)}, u32[]{:S(2)}, u32[]{:S(2)}) collective-permute-start(bf16[128,4224]{1,0:T(8,128)(2,1)S(1)} %get-tuple-element.16.pack_ref), channel_id=1, source_target_pairs={{32,64},{96,128},{160,192},{224,256},{288,320},{352,384},{416,448}... | collective-permute-start | bytes 3244040 | tf_op jit(solution)/shard_map/ppermute | solution.py:498
  11.3 19.9 %all-to-all-start = ((bf16[32,4,2048]{2,1,0:T(4,128)(2,1)}), bf16[32,4,2048]{2,1,0:T(4,128)(2,1)S(1)}, u32[]{:S(2)}, u32[]{:S(2)}) async-start(bf16[32,4,2048]{2,1,0:T(4,128)(2,1)} %get-tuple-element.17), calls=%async_computation | async-start | bytes 1048576 | tf_op jit(solution)/shard_map/all_to_all | solution.py:523
  33.6 15.3 %all-to-all-start.1 = ((bf16[32,4,2048]{2,1,0:T(4,128)(2,1)}), bf16[32,4,2048]{2,1,0:T(4,128)(2,1)S(1)}, u32[]{:S(2)}, u32[]{:S(2)}) async-start(bf16[32,4,2048]{2,1,0:T(4,128)(2,1)} %get-tuple-element.23), calls=%async_computation.1 | async-start | bytes 1048576 | tf_op jit(solution)/shard_map/all_to_all | solution.py:523
